TPU v7x, 32 devices: a whole 2x2x4 slice. The times are simulated.
32 devices in a mesh: member: 4 (over y, x), slab: 8 (over z, core).
Axes of the slice: x: 2, y: 2, z: 4, core: 2. Of those that a mesh axis runs over, the one named last changes fastest.
Arguments:
- control: float32 [16, 2, 1024, 2048], P('member', None, 'slab'), may hold values from -6 to 6
- perturbation: bfloat16 [16, 2, 1024, 2048], P('member', None, 'slab'), may hold values from -6 to 6
- loc_row: float32 [2, 1024], P(None, 'slab'), may hold values from 0.2 to 2
- loc_col: float32 [2, 2048], replicated, may hold values from 0.2 to 2
- obs_tile: int32 [2048], P('slab'), may hold values from 0 to 4095, as said below
- obs_count: int32 [2048], P('slab'), may hold values from 1 to 128
- obs_value: float32 [2048, 128], P('slab'), may hold values from -12 to 12
Outputs:
- gradient: float32 [16, 2, 1024, 2048], P('member', None, 'slab')
Inputs may be any that keep to these rules, and one draw needn't show every extreme that they name: `obs_tile`: entry i names a tile of slab block i // 256 in that block's numbering, whose columns lie in column share k = (i mod 256) // (256 / 8), i.e. columns k * 2048 / 8 onward; tiles may repeat. cells 0 to obs_count - 1 of a tile are observed.
All inputs are finite; a program needn't handle non-finite values.
Results may differ from a plain program's by a relative error of at most 0.012.
Values may be sent and summed in bfloat16 or wider, within the bound.
A program may use at most 64 MiB of HBM per device.

v0:
```python
import jax
import jax.numpy as jnp
from jax import lax
from jax.sharding import PartitionSpec as P

TILE = 128


def hartley(order):
    index = jnp.arange(order, dtype=jnp.int32)
    product = index[:, None] * index[None, :] % order
    angle = 2.0 * jnp.pi * product.astype(jnp.float32) / order
    table = (jnp.cos(angle) + jnp.sin(angle)) / jnp.sqrt(jnp.float32(order))
    return table.astype(jnp.bfloat16)


def shards(control, perturbation, loc_row, loc_col, obs_tile, obs_count, obs_value):
    members, levels, rows, width = control.shape
    slabs = lax.axis_size("slab")
    height = rows * slabs
    share = width // slabs
    table_y = hartley(height)
    table_x = hartley(width)
    amplitude = loc_row[:, :, None] * loc_col[:, None, :]

    def columns_pass(block):
        product = jnp.einsum("ya,mlac->mlyc", table_y, block, preferred_element_type=jnp.float32)
        return product.astype(jnp.bfloat16)

    scaled = (control * amplitude[None]).astype(jnp.bfloat16)
    along = jnp.dot(scaled.reshape(-1, width), table_x, preferred_element_type=jnp.float32)
    along = along.astype(jnp.bfloat16).reshape(members, levels, rows, width)
    field_cols = columns_pass(
        lax.all_to_all(along, "slab", split_axis=3, concat_axis=2, tiled=True)
    )
    tile_total = levels * rows * (width // TILE)
    all_tiles = lax.all_gather(obs_tile, "slab", axis=0, tiled=True)
    per_peer = obs_tile.shape[0] // slabs
    mine = lax.axis_index("slab")
    listed = lax.dynamic_slice_in_dim(all_tiles.reshape(slabs, slabs, per_peer), mine, 1, 1)
    listed = listed.reshape(slabs, per_peer)
    per_row = width // TILE
    level = listed // (rows * per_row)
    row_in = listed // per_row % rows
    local_tile = listed % per_row - mine * (share // TILE)
    source = jnp.arange(slabs, dtype=jnp.int32)[:, None]
    flat_index = ((level * height + source * rows + row_in) * (share // TILE) + local_tile).reshape(
        -1
    )
    picked = field_cols.reshape(members, -1, TILE)[:, flat_index]
    field_obs = lax.all_to_all(picked, "slab", split_axis=1, concat_axis=1, tiled=True)
    pert_obs = perturbation.reshape(members, -1, TILE)[:, obs_tile].astype(jnp.float32)
    partial_obs = jnp.sum(pert_obs * field_obs.astype(jnp.float32), axis=0)
    cells = lax.psum(partial_obs, "member")
    resid = cells - obs_value
    observed = jnp.arange(TILE, dtype=jnp.int32)[None, :] < obs_count[:, None]
    score = jnp.where(observed, resid / jnp.sqrt(1.0 + resid * resid / 4.0), 0.0)
    adjoint_tiles = jnp.zeros((tile_total, TILE), jnp.float32).at[obs_tile].add(score)
    weighted_obs = (pert_obs * adjoint_tiles[obs_tile][None]).astype(jnp.bfloat16)
    arrived = lax.all_to_all(weighted_obs, "slab", split_axis=1, concat_axis=1, tiled=True)
    empty = jnp.zeros((members, levels * height * (share // TILE), TILE), jnp.bfloat16)
    filled = empty.at[:, flat_index].set(arrived)
    back_cols = columns_pass(filled.reshape(members, levels, height, share))
    back = lax.all_to_all(back_cols, "slab", split_axis=2, concat_axis=3, tiled=True)
    result = jnp.dot(back.reshape(-1, width), table_x, preferred_element_type=jnp.float32)
    return result.reshape(members, levels, rows, width) * amplitude[None]


def solution(mesh):
    placed = (
        P("member", None, "slab", None),
        P("member", None, "slab", None),
        P(None, "slab"),
        P(),
        P("slab"),
        P("slab"),
        P("slab", None),
    )
    return jax.shard_map(
        shards,
        mesh=mesh,
        in_specs=placed,
        out_specs=P("member", None, "slab", None),
        check_vma=False,
    )
```

profile of v0, /device:TPU:0, one launch (start us, length us, event | category | flops | bytes accessed | tf_op | source)
XLA Modules:
  0.0 563.9 jit_solution(10304791134085167966)
XLA Ops:
  6.5 68.2 %multiply_convert_fusion.9 = bf16[2048,2048]{1,0:T(8,128)(2,1)} fusion(), kind=kLoop, calls=%fused_computation.11.clone.1.clone.clone.clone.1 | loop fusion | flops 71303168 | bytes 8388608 | tf_op jit(solution)/shard_map/dot_general | solution.py:31
  74.7 0.0 copy-done.2
  74.7 0.0 copy-done.5
  74.7 0.2 broadcast_multiply_fusion
  74.9 0.0 copy-done
  74.9 1.4 multiply_convert_fusion.3
  76.4 12.6 %fusion.18 = bf16[1024,2048]{1,0:T(8,128)(2,1)} fusion(bf16[1024,2048]{1,0:T(8,128)(2,1)S(1)} %bitcast.61, bf16[2048,2048]{1,0:T(8,128)(2,1)} %multiply_convert_fusion.9), kind=kOutput, calls=%fused_computation.34 | convolution fusion | flops 8592031744 | bytes 16777216 | tf_op jit(solution)/shard_map/dot_general | solution.py:31
  89.0 11.1 %copy.24 = bf16[4,2,128,2048]{2,1,0,3:T(2,128)(2,1)} copy(bf16[4,2,128,2048]{3,2,1,0:T(8,128)(2,1)} %bitcast.62) | data formatting | bytes 8388608 | tf_op jit(solution)/shard_map/reshape | solution.py:32
  100.1 6.5 %all-to-all-start = ((bf16[4,2,128,2048]{2,1,0,3:T(2,128)(2,1)}), bf16[4,2,128,2048]{2,1,0,3:T(2,128)(2,1)}, u32[]{:S(2)}, u32[]{:S(2)}) async-start(bf16[4,2,128,2048]{2,1,0,3:T(2,128)(2,1)} %copy.24), calls=%async_computation | async-start | bytes 8388608 | tf_op jit(solution)/shard_map/all_to_all | solution.py:34
  106.6 75.3 %all-gather = s32[8,1,256]{2,1,0:T(1,128)S(1)} all-gather(s32[1,1,256]{2,1,0:T(1,128)S(1)} %bitcast.66), channel_id=1, replica_groups=mesh['member'=4,'slab'=8] {'slab'}, dimensions={0}, use_global_device_ids=true | all-gather | bytes 9216 | tf_op jit(solution)/shard_map/all_gather | solution.py:37
  181.9 0.1 reshape.231
  182.0 0.1 reshape.232
  182.1 0.1 add.140
  182.1 0.1 add.141
  182.3 18.5 %all-to-all-done = bf16[4,2,128,2048]{2,1,0,3:T(2,128)(2,1)} async-done(((bf16[4,2,128,2048]{2,1,0,3:T(2,128)(2,1)}), bf16[4,2,128,2048]{2,1,0,3:T(2,128)(2,1)}, u32[]{:S(2)}, u32[]{:S(2)}) %all-to-all-start) | async-done | bytes 4194336 | tf_op jit(solution)/shard_map/all_to_all | solution.py:34
  200.7 6.9 %copy.38 = bf16[4,2,128,8,256]{2,3,4,1,0:T(8,128)(2,1)} copy(bf16[4,2,128,8,256]{2,1,0,4,3:T(2,128)(2,1)} %bitcast.5) | data formatting | bytes 8388608 | tf_op jit(solution)/shard_map/all_to_all | solution.py:34
  207.6 7.3 %all_to_all.33 = bf16[4,2,1024,256]{2,3,1,0:T(8,128)(2,1)} reshape(bf16[4,2,8,128,256]{3,2,4,1,0:T(8,128)(2,1)} %bitcast.59) | data formatting | bytes 8388608 | tf_op jit(solution)/shard_map/all_to_all | solution.py:34
  214.9 23.3 %convert_bitcast_fusion.1 = bf16[4,2,1024,256]{2,3,1,0:T(8,128)(2,1)} fusion(bf16[4,2,1024,256]{2,3,1,0:T(8,128)(2,1)} %all_to_all.33), kind=kOutput, calls=%fused_computation.29 | convolution fusion | flops 4314890240 | bytes 8388608 | tf_op jit(solution)/shard_map/ya,mlac->mlyc/dot_general | solution.py:27
  238.2 6.2 %copy.26 = bf16[4,2,1024,256]{3,2,1,0:T(8,128)(2,1)} copy(bf16[4,2,1024,256]{2,3,1,0:T(8,128)(2,1)} %convert_bitcast_fusion.1) | data formatting | bytes 8388608 | tf_op jit(solution)/shard_map/convert_element_type | solution.py:28
  244.4 7.1 %reshape.236 = bf16[4,4096,128]{2,1,0:T(8,128)(2,1)} reshape(bf16[4,2,1024,256]{3,2,1,0:T(8,128)(2,1)} %copy.26) | data formatting | bytes 8388608 | tf_op jit(solution)/shard_map/reshape | solution.py:50
  251.5 7.6 %copy.27 = bf16[4,4096,128]{2,0,1:T(4,128)(2,1)} copy(bf16[4,4096,128]{2,1,0:T(8,128)(2,1)} %reshape.236) | data formatting | bytes 8388608 | tf_op jit(solution)/shard_map/reshape | solution.py:50
  259.1 3.8 gather_fusion.1
  262.9 6.0 %all-to-all-start.1 = ((bf16[4,256,128]{2,0,1:T(4,128)(2,1)}), bf16[4,256,128]{2,0,1:T(4,128)(2,1)S(1)}, u32[]{:S(2)}, u32[]{:S(2)}) async-start(bf16[4,256,128]{2,0,1:T(4,128)(2,1)} %bitcast.10), calls=%async_computation.1 | async-start | bytes 524288 | tf_op jit(solution)/shard_map/all_to_all | solution.py:51
  268.9 0.2 all-reduce.2.cloned.1.call-start
  269.1 7.4 %reshape.233 = bf16[4,4096,128]{2,1,0:T(8,128)(2,1)} reshape(bf16[4,2,128,2048]{3,2,1,0:T(8,128)(2,1)} %param.8) | data formatting | bytes 8388608 | tf_op jit(solution)/shard_map/reshape | solution.py:52
  276.5 7.6 %copy.23 = bf16[4,4096,128]{2,0,1:T(4,128)(2,1)} copy(bf16[4,4096,128]{2,1,0:T(8,128)(2,1)} %reshape.233) | data formatting | bytes 8388608 | tf_op jit(solution)/shard_map/reshape | solution.py:52
  284.1 3.2 gather_fusion
  287.3 0.0 all-to-all-done.1
  287.3 1.0 fusion.30
  288.4 0.0 all-reduce.2.cloned.1.call-update
  288.4 43.8 %all-reduce.2.cloned.1.call-done = f32[256,128]{1,0:T(8,128)} async-done(((f32[256,128]{1,0:T(8,128)}), f32[256,128]{1,0:T(8,128)}) %all-reduce.2.cloned.1.call-update) | async-done | bytes 131088 | tf_op jit(solution)/shard_map/psum | solution.py:54
  332.2 0.0 copy-done.1
  332.2 3.3 scatter_custom_fusion
  335.5 2.3 gather_fusion.2
  337.8 0.1 fusion.31
  337.9 14.1 %all_to_all.43 = bf16[4,256,128]{2,0,1:T(4,128)(2,1)S(1)} all-to-all(bf16[4,256,128]{2,0,1:T(4,128)(2,1)S(1)} %fusion.31), channel_id=1, replica_groups=mesh['member'=4,'slab'=8] {'slab'}, dimensions={1} | all-to-all | bytes 524288 | tf_op jit(solution)/shard_map/all_to_all | solution.py:60
  352.0 2.8 broadcast_in_dim.9
  354.9 28.1 %scatter_fusion = bf16[4,4096,128]{2,0,1:T(4,128)(2,1)} fusion(bf16[4,4096,128]{2,0,1:T(4,128)(2,1)} %broadcast_in_dim.9, s32[256]{0:T(256)S(1)} %bitcast.65, bf16[256,4,128]{2,1,0:T(4,128)(2,1)S(1)} %bitcast.63), kind=kCustom, calls=%fused_computation.4 | custom fusion | bytes 787456 | tf_op jit(solution)/shard_map/scatter | solution.py:62
  382.9 4.7 copy.28
  387.6 7.1 %reshape.237 = bf16[4,2,1024,256]{3,2,1,0:T(8,128)(2,1)} reshape(bf16[4,4096,128]{2,1,0:T(8,128)(2,1)} %copy.28) | data formatting | bytes 8388608 | tf_op jit(solution)/shard_map/reshape | solution.py:63
  394.7 23.8 %convert_bitcast_fusion = bf16[4,2,1024,256]{2,3,1,0:T(8,128)(2,1)} fusion(bf16[4,2,1024,256]{3,2,1,0:T(8,128)(2,1)} %reshape.237), kind=kOutput, calls=%fused_computation.28 | convolution fusion | flops 4314890240 | bytes 8388608 | tf_op jit(solution)/shard_map/ya,mlac->mlyc/dot_general | solution.py:27
  418.4 11.1 %copy.30 = bf16[4,2,1024,256]{3,1,0,2:T(2,128)(2,1)} copy(bf16[4,2,1024,256]{2,3,1,0:T(8,128)(2,1)} %convert_bitcast_fusion) | data formatting | bytes 8388608 | tf_op jit(solution)/shard_map/convert_element_type | solution.py:28
  429.6 4.8 all-to-all-start.3
  434.4 68.2 %fusion.75 = bf16[2048,2048,1,1]{1,0,3,2:T(8,128)(2,1)} fusion(), kind=kLoop, calls=%fused_computation.16.clone.clone.clone.1 | loop fusion | flops 71303168 | bytes 8388608 | tf_op jit(solution)/shard_map/dot_general | solution.py:65
  502.6 25.8 %all-to-all-done.3 = bf16[4,2,1024,256]{3,1,0,2:T(2,128)(2,1)} async-done(((bf16[4,2,1024,256]{3,1,0,2:T(2,128)(2,1)}), bf16[4,2,1024,256]{3,1,0,2:T(2,128)(2,1)}, u32[]{:S(2)}, u32[]{:S(2)}) %all-to-all-start.3) | async-done | bytes 4194336 | tf_op jit(solution)/shard_map/all_to_all | solution.py:64
  528.4 6.6 %copy.37 = bf16[4,2,8,128,256]{4,2,3,1,0:T(8,128)(2,1)} copy(bf16[4,2,8,128,256]{4,1,0,3,2:T(2,128)(2,1)} %bitcast.13) | data formatting | bytes 8388608 | tf_op jit(solution)/shard_map/all_to_all | solution.py:64
  534.9 7.4 %dot_general.17 = bf16[4,2,128,2048]{3,2,1,0:T(8,128)(2,1)} reshape(bf16[4,2,128,8,256]{4,3,2,1,0:T(8,128)(2,1)} %bitcast.60) | data formatting | bytes 8388608 | tf_op jit(solution)/shard_map/dot_general | solution.py:65
  542.3 14.5 %fusion.9 = f32[4,2,128,2048]{3,2,1,0:T(8,128)} fusion(bf16[4,2,128,2048]{3,2,1,0:T(8,128)(2,1)} %dot_general.17, f32[2,128,2048]{2,1,0:T(8,128)S(1)} %broadcast_multiply_fusion, bf16[2048,2048,1,1]{1,0,3,2:T(8,128)(2,1)} %fusion.75), kind=kOutput, calls=%fused_computation.22 | convolution fusion | flops 8592031744 | bytes 23068672 | tf_op jit(solution)/shard_map/dot_general | solution.py:65
  (15 shorter events, 0.1 us)
Async XLA Ops:
  6.5 68.2 %copy-start.2 = (f32[2,2048]{1,0:T(2,128)S(1)}, f32[2,2048]{1,0:T(2,128)}, u32[]{:S(2)}) copy-start(f32[2,2048]{1,0:T(2,128)} %param.10) | copy-start | bytes 49156
  6.5 68.2 %copy-start.5 = (f32[2,128]{1,0:T(2,128)S(1)}, f32[2,128]{1,0:T(2,128)}, u32[]{:S(2)}) copy-start(f32[2,128]{1,0:T(2,128)} %param.9) | copy-start | bytes 3076
  6.5 68.4 %copy-start = (f32[4,2,128,2048]{3,2,1,0:T(8,128)S(1)}, f32[4,2,128,2048]{3,2,1,0:T(8,128)}, u32[]{:S(2)}) copy-start(f32[4,2,128,2048]{3,2,1,0:T(8,128)} %param.7) | copy-start | bytes 25165828
  100.1 6.5 %copy-start.3 = (s32[256]{0:T(256)S(1)}, s32[256]{0:T(256)}, u32[]{:S(2)}) copy-start(s32[256]{0:T(256)} %param.11) | copy-start | bytes 3076
  100.1 100.6 %all-to-all-start = ((bf16[4,2,128,2048]{2,1,0,3:T(2,128)(2,1)}), bf16[4,2,128,2048]{2,1,0,3:T(2,128)(2,1)}, u32[]{:S(2)}, u32[]{:S(2)}) async-start(bf16[4,2,128,2048]{2,1,0,3:T(2,128)(2,1)} %copy.24), calls=%async_computation | async-start | bytes 8388608 | tf_op jit(solution)/shard_map/all_to_all | solution.py:34
  262.9 24.4 %all-to-all-start.1 = ((bf16[4,256,128]{2,0,1:T(4,128)(2,1)}), bf16[4,256,128]{2,0,1:T(4,128)(2,1)S(1)}, u32[]{:S(2)}, u32[]{:S(2)}) async-start(bf16[4,256,128]{2,0,1:T(4,128)(2,1)} %bitcast.10), calls=%async_computation.1 | async-start | bytes 524288 | tf_op jit(solution)/shard_map/all_to_all | solution.py:51
  268.9 63.3 %all-reduce.2.cloned.1.call-start = ((), (), s32[]{:S(2)}) async-start(), calls=%async_computation.4 | async-start | bytes 262144 | tf_op jit(solution)/shard_map/psum | solution.py:54
  276.5 55.7 %copy-start.1 = (f32[256,128]{1,0:T(8,128)S(1)}, f32[256,128]{1,0:T(8,128)}, u32[]{:S(2)}) copy-start(f32[256,128]{1,0:T(8,128)} %param.13) | copy-start | bytes 393220
  276.5 55.7 %copy-start.4 = (s32[256]{0:T(256)S(1)}, s32[256]{0:T(256)}, u32[]{:S(2)}) copy-start(s32[256]{0:T(256)} %param.12) | copy-start | bytes 3076
  429.6 98.8 %all-to-all-start.3 = ((bf16[4,2,1024,256]{3,1,0,2:T(2,128)(2,1)}), bf16[4,2,1024,256]{3,1,0,2:T(2,128)(2,1)}, u32[]{:S(2)}, u32[]{:S(2)}) async-start(bf16[4,2,1024,256]{3,1,0,2:T(2,128)(2,1)} %copy.30), calls=%async_computation.3 | async-start | bytes 8388608 | tf_op jit(solution)/shard_map/all_to_all | solution.py:64
Sparse Core Ops, SparseCore 0:
  288.5 43.6 all-reduce.1
where the time goes:
time: 572 us; the launch traced here: 564 us
  other arithmetic  142 us (25%)
  local copies, waits for them, and re-layouts  139 us (24%)
  blocking collectives  89.4 us (16%)
  waiting for transfers between devices  88.1 us (15%)
  matrix products  74.1 us (13%)
  starting transfers between devices  17.5 us (3%)
  between operations  13.7 us (2%)
    all_gather x1, blocking collectives, shards(): all_tiles = lax.all_gather(obs_tile, 'slab', axis=0, tiled=True)  75.3 us
    dot_general x1, other arithmetic, shards(): jnp.dot(back.reshape(-1, width), table_x, preferred_element_type=jnp.floa...  68.2 us
    dot_general x1, other arithmetic, shards(): jnp.dot(scaled.reshape(-1, width), table_x, preferred_element_type=jnp.fl...  68.2 us
    dot_general x2, matrix products, columns_pass(): jnp.einsum('ya,mlac->mlyc', table_y, block, preferred_element_type=jnp.fl...  47.1 us
    psum x1, waiting for transfers between devices, shards(): cells = lax.psum(partial_obs, 'member')  43.8 us
    scatter x2, local copies, waits for them, and re-layouts, shards(): filled = empty.at[:, flat_index].set(arrived)  32.7 us
    all_to_all x1, waiting for transfers between devices, shards(): lax.all_to_all(back_cols, 'slab', split_axis=2, concat_axis=3, tiled=True)  25.8 us
    all_to_all x1, waiting for transfers between devices, shards(): lax.all_to_all(along, 'slab', split_axis=3, concat_axis=2, tiled=True)  18.5 us
  transfers between devices with their start and end apart: 4, of which 3 were waited for; matrix products, arithmetic and copies ran while one was open for 15% of the time, Pallas kernels for 0%

commit v1 on v0

--- a/solution.py
+++ b/solution.py
@@ -51,7 +51,9 @@
     field_obs = lax.all_to_all(picked, "slab", split_axis=1, concat_axis=1, tiled=True)
     pert_obs = perturbation.reshape(members, -1, TILE)[:, obs_tile].astype(jnp.float32)
     partial_obs = jnp.sum(pert_obs * field_obs.astype(jnp.float32), axis=0)
-    cells = lax.psum(partial_obs, "member")
+    cells = partial_obs
+    for hop in (1, 2):
+        cells = cells + lax.ppermute(cells, "member", [(dev, dev ^ hop) for dev in range(4)])
     resid = cells - obs_value
     observed = jnp.arange(TILE, dtype=jnp.int32)[None, :] < obs_count[:, None]
     score = jnp.where(observed, resid / jnp.sqrt(1.0 + resid * resid / 4.0), 0.0)

time: 572 us -> 525 us (0.918)
  waiting for transfers between devices: 88.1 us -> 52.2 us
  between operations: 13.7 us -> 0.34 us
    psum x1 -> x0, waiting for transfers between devices: 43.8 us -> none  [shards(): cells = lax.psum(partial_obs, 'member')]
    ppermute x0 -> x2, waiting for transfers between devices: none -> 7.93 us  [shards(): lax.ppermute(cells, 'member', [(dev, dev ^ hop) for dev in range(4)])]
  transfers between devices with their start and end apart: 4 -> 5, of which waited for: 3 -> 4; matrix products, arithmetic and copies ran while one was open for 15% -> 17% of each run, Pallas kernels for 0% -> 0%
where the time goes in v1:
time: 525 us; the launch traced here: 517 us
  other arithmetic  141 us (27%)
  local copies, waits for them, and re-layouts  139 us (26%)
  blocking collectives  89.4 us (17%)
  matrix products  74.1 us (14%)
  waiting for transfers between devices  52.2 us (10%)
  starting transfers between devices  20.7 us (4%)
    all_gather x1, blocking collectives, shards(): all_tiles = lax.all_gather(obs_tile, 'slab', axis=0, tiled=True)  75.3 us
    dot_general x1, other arithmetic, shards(): jnp.dot(back.reshape(-1, width), table_x, preferred_element_type=jnp.floa...  68.2 us
    dot_general x1, other arithmetic, shards(): jnp.dot(scaled.reshape(-1, width), table_x, preferred_element_type=jnp.fl...  68.2 us
    dot_general x2, matrix products, columns_pass(): jnp.einsum('ya,mlac->mlyc', table_y, block, preferred_element_type=jnp.fl...  47 us
    scatter x2, local copies, waits for them, and re-layouts, shards(): filled = empty.at[:, flat_index].set(arrived)  32.7 us
    all_to_all x1, waiting for transfers between devices, shards(): lax.all_to_all(back_cols, 'slab', split_axis=2, concat_axis=3, tiled=True)  25.8 us
    all_to_all x1, waiting for transfers between devices, shards(): lax.all_to_all(along, 'slab', split_axis=3, concat_axis=2, tiled=True)  18.5 us
    convert_element_type x2, local copies, waits for them, and re-layouts, columns_pass(): return product.astype(jnp.bfloat16)  17.4 us
  transfers between devices with their start and end apart: 5, of which 4 were waited for; matrix products, arithmetic and copies ran while one was open for 17% of the time, Pallas kernels for 0%

profile of v1, /device:TPU:0, one launch (start us, length us, event | category | flops | bytes accessed | tf_op | source)
XLA Modules:
  0.0 516.8 jit_solution(6150510926545033937)
XLA Ops:
  0.0 68.2 %multiply_convert_fusion.9 = bf16[2048,2048]{1,0:T(8,128)(2,1)} fusion(), kind=kLoop, calls=%fused_computation.11.clone.1.clone.clone.clone.1 | loop fusion | flops 71303168 | bytes 8388608 | tf_op jit(solution)/shard_map/dot_general | solution.py:31
  68.2 0.0 copy-done.4
  68.2 0.2 broadcast_multiply_fusion
  68.4 1.4 multiply_convert_fusion.3
  69.8 12.6 %fusion.18 = bf16[1024,2048]{1,0:T(8,128)(2,1)} fusion(bf16[1024,2048]{1,0:T(8,128)(2,1)S(1)} %bitcast.61, bf16[2048,2048]{1,0:T(8,128)(2,1)} %multiply_convert_fusion.9), kind=kOutput, calls=%fused_computation.34 | convolution fusion | flops 8592031744 | bytes 16777216 | tf_op jit(solution)/shard_map/dot_general | solution.py:31
  82.4 11.1 %copy.24 = bf16[4,2,128,2048]{2,1,0,3:T(2,128)(2,1)} copy(bf16[4,2,128,2048]{3,2,1,0:T(8,128)(2,1)} %bitcast.62) | data formatting | bytes 8388608 | tf_op jit(solution)/shard_map/reshape | solution.py:32
  93.6 6.5 %all-to-all-start = ((bf16[4,2,128,2048]{2,1,0,3:T(2,128)(2,1)}), bf16[4,2,128,2048]{2,1,0,3:T(2,128)(2,1)}, u32[]{:S(2)}, u32[]{:S(2)}) async-start(bf16[4,2,128,2048]{2,1,0,3:T(2,128)(2,1)} %copy.24), calls=%async_computation | async-start | bytes 8388608 | tf_op jit(solution)/shard_map/all_to_all | solution.py:34
  100.0 0.0 copy-done.3
  100.1 75.3 %all-gather = s32[8,1,256]{2,1,0:T(1,128)S(1)} all-gather(s32[1,1,256]{2,1,0:T(1,128)S(1)} %bitcast.66), channel_id=1, replica_groups=mesh['member'=4,'slab'=8] {'slab'}, dimensions={0}, use_global_device_ids=true | all-gather | bytes 9216 | tf_op jit(solution)/shard_map/all_gather | solution.py:37
  175.3 0.1 reshape.231
  175.4 0.1 reshape.232
  175.5 0.1 add.144
  175.6 0.1 add.145
  175.7 18.5 %all-to-all-done = bf16[4,2,128,2048]{2,1,0,3:T(2,128)(2,1)} async-done(((bf16[4,2,128,2048]{2,1,0,3:T(2,128)(2,1)}), bf16[4,2,128,2048]{2,1,0,3:T(2,128)(2,1)}, u32[]{:S(2)}, u32[]{:S(2)}) %all-to-all-start) | async-done | bytes 4194336 | tf_op jit(solution)/shard_map/all_to_all | solution.py:34
  194.2 6.9 %copy.38 = bf16[4,2,128,8,256]{2,3,4,1,0:T(8,128)(2,1)} copy(bf16[4,2,128,8,256]{2,1,0,4,3:T(2,128)(2,1)} %bitcast.5) | data formatting | bytes 8388608 | tf_op jit(solution)/shard_map/all_to_all | solution.py:34
  201.1 7.3 %all_to_all.33 = bf16[4,2,1024,256]{2,3,1,0:T(8,128)(2,1)} reshape(bf16[4,2,8,128,256]{3,2,4,1,0:T(8,128)(2,1)} %bitcast.59) | data formatting | bytes 8388608 | tf_op jit(solution)/shard_map/all_to_all | solution.py:34
  208.4 23.3 %convert_bitcast_fusion.1 = bf16[4,2,1024,256]{2,3,1,0:T(8,128)(2,1)} fusion(bf16[4,2,1024,256]{2,3,1,0:T(8,128)(2,1)} %all_to_all.33), kind=kOutput, calls=%fused_computation.29 | convolution fusion | flops 4314890240 | bytes 8388608 | tf_op jit(solution)/shard_map/ya,mlac->mlyc/dot_general | solution.py:27
  231.7 6.2 %copy.26 = bf16[4,2,1024,256]{3,2,1,0:T(8,128)(2,1)} copy(bf16[4,2,1024,256]{2,3,1,0:T(8,128)(2,1)} %convert_bitcast_fusion.1) | data formatting | bytes 8388608 | tf_op jit(solution)/shard_map/convert_element_type | solution.py:28
  237.9 7.1 %reshape.236 = bf16[4,4096,128]{2,1,0:T(8,128)(2,1)} reshape(bf16[4,2,1024,256]{3,2,1,0:T(8,128)(2,1)} %copy.26) | data formatting | bytes 8388608 | tf_op jit(solution)/shard_map/reshape | solution.py:50
  245.0 7.6 %copy.27 = bf16[4,4096,128]{2,0,1:T(4,128)(2,1)} copy(bf16[4,4096,128]{2,1,0:T(8,128)(2,1)} %reshape.236) | data formatting | bytes 8388608 | tf_op jit(solution)/shard_map/reshape | solution.py:50
  252.6 3.9 gather_fusion.1
  256.4 6.2 %all-to-all-start.1 = ((bf16[4,256,128]{2,0,1:T(4,128)(2,1)}), bf16[4,256,128]{2,0,1:T(4,128)(2,1)S(1)}, u32[]{:S(2)}, u32[]{:S(2)}) async-start(bf16[4,256,128]{2,0,1:T(4,128)(2,1)} %bitcast.10), calls=%async_computation.1 | async-start | bytes 524288 | tf_op jit(solution)/shard_map/all_to_all | solution.py:51
  262.6 7.4 %reshape.233 = bf16[4,4096,128]{2,1,0:T(8,128)(2,1)} reshape(bf16[4,2,128,2048]{3,2,1,0:T(8,128)(2,1)} %param.8) | data formatting | bytes 8388608 | tf_op jit(solution)/shard_map/reshape | solution.py:52
  270.0 7.6 %copy.23 = bf16[4,4096,128]{2,0,1:T(4,128)(2,1)} copy(bf16[4,4096,128]{2,1,0:T(8,128)(2,1)} %reshape.233) | data formatting | bytes 8388608 | tf_op jit(solution)/shard_map/reshape | solution.py:52
  277.6 3.2 gather_fusion
  280.8 0.0 all-to-all-done.1
  280.8 0.4 fusion.30
  281.2 1.6 collective-permute-start
  282.8 4.4 collective-permute-done
  287.2 1.6 collective-permute-start.1
  288.8 3.5 collective-permute-done.1
  292.3 0.0 copy-done.1
  292.3 2.9 scatter_custom_fusion
  295.2 2.3 gather_fusion.2
  297.5 0.1 fusion.31
  297.7 14.1 %all_to_all.43 = bf16[4,256,128]{2,0,1:T(4,128)(2,1)S(1)} all-to-all(bf16[4,256,128]{2,0,1:T(4,128)(2,1)S(1)} %fusion.31), channel_id=1, replica_groups=mesh['member'=4,'slab'=8] {'slab'}, dimensions={1} | all-to-all | bytes 524288 | tf_op jit(solution)/shard_map/all_to_all | solution.py:62
  311.8 2.8 broadcast_in_dim.9
  314.6 28.1 %scatter_fusion = bf16[4,4096,128]{2,0,1:T(4,128)(2,1)} fusion(bf16[4,4096,128]{2,0,1:T(4,128)(2,1)} %broadcast_in_dim.9, s32[256]{0:T(256)S(1)} %bitcast.65, bf16[256,4,128]{2,1,0:T(4,128)(2,1)S(1)} %bitcast.63), kind=kCustom, calls=%fused_computation.4 | custom fusion | bytes 787456 | tf_op jit(solution)/shard_map/scatter | solution.py:64
  342.7 4.7 copy.28
  347.4 7.1 %reshape.237 = bf16[4,2,1024,256]{3,2,1,0:T(8,128)(2,1)} reshape(bf16[4,4096,128]{2,1,0:T(8,128)(2,1)} %copy.28) | data formatting | bytes 8388608 | tf_op jit(solution)/shard_map/reshape | solution.py:65
  354.4 23.8 %convert_bitcast_fusion = bf16[4,2,1024,256]{2,3,1,0:T(8,128)(2,1)} fusion(bf16[4,2,1024,256]{3,2,1,0:T(8,128)(2,1)} %reshape.237), kind=kOutput, calls=%fused_computation.28 | convolution fusion | flops 4314890240 | bytes 8388608 | tf_op jit(solution)/shard_map/ya,mlac->mlyc/dot_general | solution.py:27
  378.2 11.1 %copy.30 = bf16[4,2,1024,256]{3,1,0,2:T(2,128)(2,1)} copy(bf16[4,2,1024,256]{2,3,1,0:T(8,128)(2,1)} %convert_bitcast_fusion) | data formatting | bytes 8388608 | tf_op jit(solution)/shard_map/convert_element_type | solution.py:28
  389.3 4.8 all-to-all-start.3
  394.2 68.2 %fusion.76 = bf16[2048,2048,1,1]{1,0,3,2:T(8,128)(2,1)} fusion(), kind=kLoop, calls=%fused_computation.16.clone.clone.clone.1 | loop fusion | flops 71303168 | bytes 8388608 | tf_op jit(solution)/shard_map/dot_general | solution.py:67
  462.3 25.8 %all-to-all-done.3 = bf16[4,2,1024,256]{3,1,0,2:T(2,128)(2,1)} async-done(((bf16[4,2,1024,256]{3,1,0,2:T(2,128)(2,1)}), bf16[4,2,1024,256]{3,1,0,2:T(2,128)(2,1)}, u32[]{:S(2)}, u32[]{:S(2)}) %all-to-all-start.3) | async-done | bytes 4194336 | tf_op jit(solution)/shard_map/all_to_all | solution.py:66
  488.1 6.6 %copy.37 = bf16[4,2,8,128,256]{4,2,3,1,0:T(8,128)(2,1)} copy(bf16[4,2,8,128,256]{4,1,0,3,2:T(2,128)(2,1)} %bitcast.13) | data formatting | bytes 8388608 | tf_op jit(solution)/shard_map/all_to_all | solution.py:66
  494.7 7.4 %dot_general.17 = bf16[4,2,128,2048]{3,2,1,0:T(8,128)(2,1)} reshape(bf16[4,2,128,8,256]{4,3,2,1,0:T(8,128)(2,1)} %bitcast.60) | data formatting | bytes 8388608 | tf_op jit(solution)/shard_map/dot_general | solution.py:67
  502.1 14.5 %fusion.9 = f32[4,2,128,2048]{3,2,1,0:T(8,128)} fusion(bf16[4,2,128,2048]{3,2,1,0:T(8,128)(2,1)} %dot_general.17, f32[2,128,2048]{2,1,0:T(8,128)S(1)} %broadcast_multiply_fusion, bf16[2048,2048,1,1]{1,0,3,2:T(8,128)(2,1)} %fusion.76), kind=kOutput, calls=%fused_computation.22 | convolution fusion | flops 8592031744 | bytes 23068672 | tf_op jit(solution)/shard_map/dot_general | solution.py:67
  (17 shorter events, 0.1 us)
Async XLA Ops:
  0.0 68.2 %copy-start.2 = (f32[2,2048]{1,0:T(2,128)S(1)}, f32[2,2048]{1,0:T(2,128)}, u32[]{:S(2)}) copy-start(f32[2,2048]{1,0:T(2,128)} %param.10) | copy-start | bytes 49156
  0.0 68.2 %copy-start.4 = (f32[2,128]{1,0:T(2,128)S(1)}, f32[2,128]{1,0:T(2,128)}, u32[]{:S(2)}) copy-start(f32[2,128]{1,0:T(2,128)} %param.9) | copy-start | bytes 3076
  0.0 68.4 %copy-start = (f32[4,2,128,2048]{3,2,1,0:T(8,128)S(1)}, f32[4,2,128,2048]{3,2,1,0:T(8,128)}, u32[]{:S(2)}) copy-start(f32[4,2,128,2048]{3,2,1,0:T(8,128)} %param.7) | copy-start | bytes 25165828
  93.6 6.5 %copy-start.3 = (s32[256]{0:T(256)S(1)}, s32[256]{0:T(256)}, u32[]{:S(2)}) copy-start(s32[256]{0:T(256)} %param.11) | copy-start | bytes 3076
  93.6 100.6 %all-to-all-start = ((bf16[4,2,128,2048]{2,1,0,3:T(2,128)(2,1)}), bf16[4,2,128,2048]{2,1,0,3:T(2,128)(2,1)}, u32[]{:S(2)}, u32[]{:S(2)}) async-start(bf16[4,2,128,2048]{2,1,0,3:T(2,128)(2,1)} %copy.24), calls=%async_computation | async-start | bytes 8388608 | tf_op jit(solution)/shard_map/all_to_all | solution.py:34
  256.4 24.4 %all-to-all-start.1 = ((bf16[4,256,128]{2,0,1:T(4,128)(2,1)}), bf16[4,256,128]{2,0,1:T(4,128)(2,1)S(1)}, u32[]{:S(2)}, u32[]{:S(2)}) async-start(bf16[4,256,128]{2,0,1:T(4,128)(2,1)} %bitcast.10), calls=%async_computation.1 | async-start | bytes 524288 | tf_op jit(solution)/shard_map/all_to_all | solution.py:51
  270.0 22.3 %copy-start.1 = (f32[256,128]{1,0:T(8,128)S(1)}, f32[256,128]{1,0:T(8,128)}, u32[]{:S(2)}) copy-start(f32[256,128]{1,0:T(8,128)} %param.13) | copy-start | bytes 393220
  270.0 22.3 %copy-start.5 = (s32[256]{0:T(256)S(1)}, s32[256]{0:T(256)}, u32[]{:S(2)}) copy-start(s32[256]{0:T(256)} %param.12) | copy-start | bytes 3076
  281.2 6.0 %collective-permute-start = (f32[256,128]{1,0:T(8,128)S(1)}, f32[256,128]{1,0:T(8,128)S(1)}, u32[]{:S(2)}, u32[]{:S(2)}) collective-permute-start(f32[256,128]{1,0:T(8,128)S(1)} %fusion.30), channel_id=1, source_target_pairs={{0,8},{8,0},{16,24},{24,16},{1,9},{9,1},{17,25},{25,17},{2,10},{10... | collective-permute-start | bytes 393224 | tf_op jit(solution)/shard_map/ppermute | solution.py:56
  287.2 5.1 collective-permute-start.1
  389.3 98.8 %all-to-all-start.3 = ((bf16[4,2,1024,256]{3,1,0,2:T(2,128)(2,1)}), bf16[4,2,1024,256]{3,1,0,2:T(2,128)(2,1)}, u32[]{:S(2)}, u32[]{:S(2)}) async-start(bf16[4,2,1024,256]{3,1,0,2:T(2,128)(2,1)} %copy.30), calls=%async_computation.3 | async-start | bytes 8388608 | tf_op jit(solution)/shard_map/all_to_all | solution.py:66
